TPU v7x, 32 devices: a whole 2x2x4 slice. The times are simulated.
32 devices in a mesh: dp: 8 (over z, x), seq: 4 (over y, core).
Axes of the slice: x: 2, y: 2, z: 4, core: 2. Of those that a mesh axis runs over, the one named last changes fastest.
Arguments:
- query_rows: bfloat16 [4096, 4096], P(('dp', 'seq')), may hold values from -60 to 60
- key_rows: bfloat16 [4096, 4096], P(('dp', 'seq')), may hold values from -5 to 5
- value_rows: bfloat16 [4096, 4096], P(('dp', 'seq')), may hold values from -12 to 12
- seg_ids: int32 [4096], P(('dp', 'seq')), may hold values from 0 to 15, as said below
- timesteps: int32 [16], replicated, may hold values from 0 to 999
- w_mod: bfloat16 [256, 4096], replicated, may hold values from -0.375 to 0.375
Outputs:
- mixed_rows: bfloat16 [4096, 4096], P(('dp', 'seq'))
Inputs may be any that keep to these rules, and one draw needn't show every extreme that they name: A row's bin is seg_ids // 2, a number below the size of dp. The 128 rows of one device hold at most 32 rows of any one bin, and for every index of seq some bin holds exactly 32 rows on each device of that index. Rows of one sample lie on many devices.
All inputs are finite; a program needn't handle non-finite values.
Results may differ from a plain program's by a relative error of at most 0.0058.
Values may be sent and summed in bfloat16 or wider, within the bound.
A program may use at most 128 MiB of HBM per device.

v0:
```python
import functools
import math

import jax
import jax.numpy as jnp
from jax import lax
from jax.experimental import pallas as pl
from jax.experimental.pallas import tpu as pltpu
from jax.sharding import PartitionSpec as P

HEAD_DIM = 128
FREQ = 256
SEG_BIN = 2


def for_sending(value):
    return jax.tree.map(lambda a: a.astype(jnp.bfloat16) if a.dtype == jnp.float32 else a, value)


def scale_rows_table(timesteps, w_mod):
    half_freq = FREQ // 2
    frequencies = jnp.exp(-math.log(10000.0) * jnp.arange(half_freq, dtype=jnp.float32) / half_freq)
    angles = timesteps.astype(jnp.float32)[:, None] * frequencies[None, :]
    embedding = jnp.concatenate([jnp.cos(angles), jnp.sin(angles)], axis=1)
    activated = jax.nn.silu(embedding).astype(jnp.bfloat16)
    return jnp.dot(activated, w_mod, preferred_element_type=jnp.float32)


def slot_places(row_bins, bin_count, capacity):
    bin_hits = (row_bins[:, None] == jnp.arange(bin_count, dtype=jnp.int32)[None, :]).astype(
        jnp.int32
    )
    ranks = jnp.cumsum(bin_hits, axis=0) - bin_hits
    slot_rank = jnp.sum(ranks * bin_hits, axis=1)
    target = row_bins * capacity + slot_rank
    return jnp.arange(bin_count * capacity, dtype=jnp.int32)[:, None] == target[None, :]


def slot_ids_of(placement, sample_ids):
    return jnp.sum(jnp.where(placement, sample_ids[None, :] + 1, 0), axis=1) - 1


def attend_slots(query_part, key_part, value_part, sample_ids):
    length, row_width = query_part.shape
    head_count = row_width // HEAD_DIM
    block_rows = min(512, length)
    score_scale = 1.0 / math.sqrt(HEAD_DIM)
    query_blocks = query_part.reshape(length // block_rows, block_rows, head_count, HEAD_DIM)
    key_heads = key_part.reshape(length, head_count, HEAD_DIM)
    value_heads = value_part.reshape(length, head_count, HEAD_DIM)
    id_blocks = sample_ids.reshape(length // block_rows, block_rows)

    def one_block(block_pair):
        query_block, query_ids = block_pair
        scores = (
            jnp.einsum("qhd,khd->hqk", query_block, key_heads, preferred_element_type=jnp.float32)
            * score_scale
        )
        same_sample = query_ids[:, None] == sample_ids[None, :]
        scores = jnp.where(same_sample[None], scores, -1e30)
        row_max = jnp.max(scores, axis=2, keepdims=True)
        weights = jnp.exp(scores - row_max)
        soft_probs = (weights / jnp.sum(weights, axis=2, keepdims=True)).astype(jnp.bfloat16)
        block_out = jnp.einsum(
            "hqk,khd->qhd", soft_probs, value_heads, preferred_element_type=jnp.float32
        )
        return block_out.astype(jnp.bfloat16).reshape(block_rows, row_width)

    return lax.map(one_block, (query_blocks, id_blocks)).reshape(length, row_width)


def place_rows(place_mask, arrays):
    return tuple(
        (
            jnp.dot(place_mask, single, preferred_element_type=jnp.float32).astype(jnp.bfloat16)
            for single in arrays
        )
    )


def routed_shards(query_rows, key_rows, value_rows, seg_ids, timesteps, w_mod):
    dp_count = lax.axis_size("dp")
    seq_count = lax.axis_size("seq")
    row_count = query_rows.shape[0]
    capacity = 2 * row_count // dp_count
    ids_tiled = jnp.broadcast_to(seg_ids[:, None], (row_count, seq_count))
    group_ids = lax.all_to_all(ids_tiled, "seq", split_axis=1, concat_axis=0, tiled=True).reshape(
        -1
    )
    head_parts = (
        lax.all_to_all(query_rows, "seq", split_axis=1, concat_axis=0, tiled=True),
        lax.all_to_all(key_rows, "seq", split_axis=1, concat_axis=0, tiled=True),
        lax.all_to_all(value_rows, "seq", split_axis=1, concat_axis=0, tiled=True),
    )
    placement = slot_places(group_ids // SEG_BIN, dp_count, seq_count * capacity)
    place_mask = placement.astype(jnp.bfloat16)
    slotted = place_rows(place_mask, head_parts)
    bin_ids = lax.all_to_all(
        slot_ids_of(placement, group_ids), "dp", split_axis=0, concat_axis=0, tiled=True
    )
    bin_query, bin_key, bin_value = jax.tree.map(
        lambda part, own: part.astype(own.dtype),
        lax.all_to_all(for_sending(slotted), "dp", split_axis=0, concat_axis=0, tiled=True),
        slotted,
    )
    attended = attend_slots(bin_query, bin_key, bin_value, bin_ids)
    returned = lax.all_to_all(attended, "dp", split_axis=0, concat_axis=0, tiled=True)
    unslotted = jnp.dot(place_mask.T, returned, preferred_element_type=jnp.float32).astype(
        jnp.bfloat16
    )
    home_rows = lax.all_to_all(unslotted, "seq", split_axis=0, concat_axis=1, tiled=True)
    scale_table = scale_rows_table(timesteps, w_mod)
    lookup = (
        seg_ids[:, None] == jnp.arange(scale_table.shape[0], dtype=jnp.int32)[None, :]
    ).astype(jnp.float32)
    row_scales = jnp.dot(
        lookup, scale_table, precision=lax.Precision.HIGHEST, preferred_element_type=jnp.float32
    )
    return (home_rows.astype(jnp.float32) * (1.0 + row_scales)).astype(jnp.bfloat16)


EXCLUDED = float(1 << 20)
NT = (((1,), (1,)), ((), ()))
TN = (((0,), (0,)), ((), ()))


def head_kernel(
    sizes,
    q_ref,
    k_ref,
    v_ref,
    ids_ref,
    table_ref,
    out_ref,
    rows_buf,
    ids_buf,
    place_buf,
    q_slots,
    k_slots,
    v_slots,
    group_out,
    out_buf,
    sem_send,
    sem_recv,
    sem_out_send,
    sem_out_recv,
):
    dp_count, seq_count, capacity, group = sizes
    count = dp_count * seq_count
    row_count = q_ref.shape[0]
    slot_count = dp_count * capacity
    me = lax.axis_index("dp") * seq_count + lax.axis_index("seq")
    sources = (k_ref, v_ref, q_ref)

    def device_of(index):
        return (index // seq_count, index % seq_count)

    half = count // 2

    def peer(away, shift):
        return ((me // half + away) % 2) * half + (me % half + shift + half) % half

    def each_peer(visit):
        @pl.loop(0, half)
        def _(shift):
            visit(1, shift)

            @pl.when(shift > 0)
            def _():
                visit(0, shift)

    def head_columns(index):
        return pl.ds(pl.multiple_of(index * HEAD_DIM, HEAD_DIM), HEAD_DIM)

    def part_copy(part, target, origin):
        return pltpu.make_async_remote_copy(
            src_ref=sources[part].at[:, head_columns(target)],
            dst_ref=rows_buf.at[origin, :, pl.ds(part * HEAD_DIM, HEAD_DIM)],
            send_sem=sem_send.at[part, target],
            recv_sem=sem_recv.at[part, origin],
            device_id=device_of(target),
            device_id_type=pl.DeviceIdType.MESH,
        )

    def ids_copy(target, origin):
        return pltpu.make_async_remote_copy(
            src_ref=ids_ref,
            dst_ref=ids_buf.at[origin],
            send_sem=sem_send.at[3, target],
            recv_sem=sem_recv.at[3, origin],
            device_id=device_of(target),
            device_id_type=pl.DeviceIdType.MESH,
        )

    def own_copy(part):
        return pltpu.make_async_copy(
            sources[part].at[:, head_columns(me)],
            rows_buf.at[me, :, pl.ds(part * HEAD_DIM, HEAD_DIM)],
            sem_recv.at[part, me],
        )

    def out_copy(target, origin):
        return pltpu.make_async_remote_copy(
            src_ref=out_buf.at[target],
            dst_ref=out_ref.at[:, head_columns(origin)],
            send_sem=sem_out_send.at[target],
            recv_sem=sem_out_recv.at[origin],
            device_id=device_of(target),
            device_id_type=pl.DeviceIdType.MESH,
        )

    def own_out():
        return pltpu.make_async_copy(
            out_buf.at[me], out_ref.at[:, head_columns(me)], sem_out_send.at[me]
        )

    for part in range(3):
        own_copy(part).start()

    barrier = pltpu.get_barrier_semaphore()

    def greet(away, shift):
        pl.semaphore_signal(
            barrier,
            inc=1,
            device_id=device_of(peer(away, shift)),
            device_id_type=pl.DeviceIdType.MESH,
        )

    each_peer(greet)
    pl.semaphore_wait(barrier, count - 1)

    def send_first(away, shift):
        target = peer(away, shift)
        ids_copy(target, me).start()
        part_copy(0, target, me).start()

    each_peer(send_first)
    for part in (1, 2):
        each_peer(lambda away, shift: part_copy(part, peer(away, shift), me).start())

    v_slots[:, :, HEAD_DIM:] = jnp.ones(
        (dp_count, count * capacity, HEAD_DIM), jnp.bfloat16
    )
    before = (
        lax.broadcasted_iota(jnp.int32, (row_count, row_count), 0)
        < lax.broadcasted_iota(jnp.int32, (row_count, row_count), 1)
    ).astype(jnp.bfloat16)
    part_lane = lax.broadcasted_iota(jnp.int32, (1, HEAD_DIM), 1) < SEG_BIN

    def member_hits(origin):
        ids = ids_buf[origin]
        member = ids - ids // SEG_BIN * SEG_BIN
        return lax.broadcasted_iota(jnp.int32, (HEAD_DIM, row_count), 0) == member

    def marks_of(place, hits):
        return lax.dot_general(
            place, hits.astype(jnp.bfloat16), NT, preferred_element_type=jnp.float32
        )

    def placed_part(place, origin, part):
        rows = rows_buf[origin, :, part * HEAD_DIM : (part + 1) * HEAD_DIM]
        return jnp.dot(place, rows, preferred_element_type=jnp.float32)

    def by_bin(value):
        return value.astype(jnp.bfloat16).reshape((dp_count, capacity, HEAD_DIM))

    def slots_at(index):
        return pl.ds(pl.multiple_of(index * capacity, capacity), capacity)

    def place_k(origin):
        bins = ids_buf[origin] // SEG_BIN
        bin_hits = lax.broadcasted_iota(jnp.int32, (16, row_count), 0) == bins
        ranks = jnp.dot(
            bin_hits.astype(jnp.bfloat16), before, preferred_element_type=jnp.float32
        )
        rank = jnp.sum(jnp.where(bin_hits, ranks, 0.0), axis=0, keepdims=True)
        slot = bins * capacity + rank.astype(jnp.int32)
        place = (
            lax.broadcasted_iota(jnp.int32, (slot_count, row_count), 0) == slot
        ).astype(jnp.bfloat16)
        place_buf[origin] = place
        other_member = marks_of(place, jnp.logical_not(member_hits(origin)))
        k_marks = jnp.where(part_lane, 1.0 - other_member, 0.0)
        k_slots[:, slots_at(origin), :HEAD_DIM] = by_bin(placed_part(place, origin, 0))
        k_slots[:, slots_at(origin), HEAD_DIM:] = by_bin(k_marks)

    def place_v(origin):
        placed = placed_part(place_buf[origin], origin, 1)
        v_slots[:, slots_at(origin), :HEAD_DIM] = by_bin(placed)

    def place_q(origin, inner):
        place = place_buf[origin]
        own_member = marks_of(place, member_hits(origin))
        q_marks = jnp.where(part_lane, (own_member - 1.0) * EXCLUDED, 0.0)
        at = slice(inner * capacity, (inner + 1) * capacity)
        q_slots[:, at, :HEAD_DIM] = by_bin(placed_part(place, origin, 2))
        q_slots[:, at, HEAD_DIM:] = by_bin(q_marks)

    ids_buf[me] = ids_ref[...]
    own_copy(0).wait()
    place_k(me)

    def take_k(away, shift):
        origin = peer(away, -shift)
        ids_copy(me, origin).wait_recv()
        part_copy(0, me, origin).wait_recv()
        place_k(origin)

    each_peer(take_k)
    own_copy(1).wait()
    place_v(me)

    def take_v(away, shift):
        origin = peer(away, -shift)
        part_copy(1, me, origin).wait_recv()
        place_v(origin)

    each_peer(take_v)

    exponent_scale = 1.0 / (math.sqrt(HEAD_DIM) * math.log(2.0))
    group_slots = group * capacity

    def attend_group(away, turn):
        for inner in range(group):
            shift = turn * group + inner
            origin = peer(away, -shift)
            if away == 0 and inner == 0:

                @pl.when(turn == 0)
                def _():
                    own_copy(2).wait()

                @pl.when(turn > 0)
                def _():
                    part_copy(2, me, origin).wait_recv()
            else:
                part_copy(2, me, origin).wait_recv()
            place_q(origin, inner)

        @pl.loop(0, dp_count, unroll=8)
        def _(bin_index):
            query = q_slots[bin_index]
            scores = lax.dot_general(
                query, k_slots[bin_index], NT, preferred_element_type=jnp.float32
            )
            row_max = jnp.max(scores, axis=1, keepdims=True)
            weights = jnp.exp2((scores - row_max) * exponent_scale).astype(jnp.bfloat16)
            sums = jnp.dot(weights, v_slots[bin_index], preferred_element_type=jnp.float32)
            attended = (sums[:, :HEAD_DIM] / sums[:, HEAD_DIM:]).astype(jnp.bfloat16)
            factor = jnp.zeros((group_slots, HEAD_DIM), jnp.float32)
            for member in range(SEG_BIN):
                mark = query[:, HEAD_DIM + member : HEAD_DIM + member + 1].astype(jnp.float32)
                row = table_ref[pl.ds(bin_index * SEG_BIN + member, 1), :]
                factor = jnp.where(mark == 0.0, 1.0 + row, factor)
            mixed = (attended.astype(jnp.float32) * factor).astype(jnp.bfloat16)
            group_out[bin_index] = mixed

        for inner in range(group):
            target = peer(away, -(turn * group + inner))
            slots = group_out[:, inner * capacity : (inner + 1) * capacity, :].reshape(
                (slot_count, HEAD_DIM)
            )
            out_buf[target] = lax.dot_general(
                place_buf[target], slots, TN, preferred_element_type=jnp.float32
            ).astype(jnp.bfloat16)
            if away == 0 and inner == 0:

                @pl.when(turn == 0)
                def _():
                    own_out().start()

                @pl.when(turn > 0)
                def _():
                    out_copy(target, me).start()
            else:
                out_copy(target, me).start()

    @pl.loop(0, half // group)
    def _(turn):
        attend_group(0, turn)
        attend_group(1, turn)

    @pl.loop(1, count)
    def _(step):
        target = (me + step) % count
        ids_copy(target, me).wait_send()
        part_copy(0, target, me).wait_send()
        part_copy(1, target, me).wait_send()
        part_copy(2, target, me).wait_send()
        out_copy(target, me).wait_send()
        out_copy(me, target).wait_recv()

    own_out().wait()


def head_shards(query_rows, key_rows, value_rows, seg_ids, timesteps, w_mod):
    dp_count = lax.axis_size("dp")
    seq_count = lax.axis_size("seq")
    count = dp_count * seq_count
    row_count, width = query_rows.shape
    capacity = 2 * row_count // dp_count
    group = count // 4
    me = lax.axis_index("dp") * seq_count + lax.axis_index("seq")
    head_weights = lax.dynamic_slice_in_dim(w_mod, me * HEAD_DIM, HEAD_DIM, 1)
    scale_table = scale_rows_table(timesteps, head_weights)
    ids = seg_ids.reshape(1, row_count)
    vmem = pl.BlockSpec(memory_space=pltpu.VMEM)
    anywhere = pl.BlockSpec(memory_space=pl.ANY)
    slots = (dp_count, count * capacity, 2 * HEAD_DIM)
    return pl.pallas_call(
        functools.partial(head_kernel, (dp_count, seq_count, capacity, group)),
        out_shape=pltpu.VMEM((row_count, width), jnp.bfloat16),
        in_specs=[anywhere, anywhere, anywhere, vmem, vmem],
        out_specs=vmem,
        scratch_shapes=[
            pltpu.VMEM((count, row_count, 3 * HEAD_DIM), jnp.bfloat16),
            pltpu.VMEM((count, 1, row_count), jnp.int32),
            pltpu.VMEM((count, dp_count * capacity, row_count), jnp.bfloat16),
            pltpu.VMEM((dp_count, group * capacity, 2 * HEAD_DIM), jnp.bfloat16),
            pltpu.VMEM(slots, jnp.bfloat16),
            pltpu.VMEM(slots, jnp.bfloat16),
            pltpu.VMEM((dp_count, group * capacity, HEAD_DIM), jnp.bfloat16),
            pltpu.VMEM((count, row_count, HEAD_DIM), jnp.bfloat16),
            pltpu.SemaphoreType.DMA((4, count)),
            pltpu.SemaphoreType.DMA((4, count)),
            pltpu.SemaphoreType.DMA((count,)),
            pltpu.SemaphoreType.DMA((count,)),
        ],
        compiler_params=pltpu.CompilerParams(
            collective_id=0, has_side_effects=True, vmem_limit_bytes=56 * 1024 * 1024
        ),
    )(query_rows, key_rows, value_rows, ids, scale_table)


def shards(query_rows, key_rows, value_rows, seg_ids, timesteps, w_mod):
    count = lax.axis_size("dp") * lax.axis_size("seq")
    whole_heads = query_rows.shape[1] == count * HEAD_DIM
    body = head_shards if whole_heads else routed_shards
    return body(query_rows, key_rows, value_rows, seg_ids, timesteps, w_mod)


def solution(mesh):
    placed = (
        P(("dp", "seq"), None),
        P(("dp", "seq"), None),
        P(("dp", "seq"), None),
        P(("dp", "seq")),
        P(),
        P(),
    )
    return jax.shard_map(
        shards, mesh=mesh, in_specs=placed, out_specs=P(("dp", "seq"), None), check_vma=False
    )
```

profile of v0, /device:TPU:7, one launch (start us, length us, event | category | flops | bytes accessed | tf_op | source)
XLA Modules:
  0.0 107.1 jit_solution(9191496236982428828)
XLA Ops:
  0.0 0.0 copy-start
  0.0 0.8 convert_element_type.6
  0.8 0.1 multiply_cosine_fusion
  0.9 0.7 copy-done
  1.6 0.7 fusion.table_ref
  2.3 103.8 %shard_map.64 = bf16[128,4096]{1,0:T(8,128)(2,1)S(1)} custom-call(bf16[128,4096]{1,0:T(8,128)(2,1)} %q_ref.1, bf16[128,4096]{1,0:T(8,128)(2,1)} %k_ref.1, bf16[128,4096]{1,0:T(8,128)(2,1)} %v_ref.1, s32[1,128]{1,0:T(1,128)} %bitcast.1, f32[16,128]{1,0:T(8,128)} %fusion.table_ref), custom_call_target="tpu_custom_call" | custom-call | tf_op jit(solution)/shard_map/pallas_call | solution.py:411
  106.2 1.0 copy.8
  (1 shorter events, 0.0 us)
Async XLA Ops:
  0.0 1.6 %copy-start = (bf16[256,4096]{1,0:T(8,128)(2,1)S(1)}, bf16[256,4096]{1,0:T(8,128)(2,1)}, u32[]{:S(2)}) copy-start(bf16[256,4096]{1,0:T(8,128)(2,1)} %param.11) | copy-start | bytes 6291460
where the time goes:
time: 108 us; the launch traced here: 107 us
  Pallas kernels  104 us (96%)
  local copies, waits for them, and re-layouts  1.64 us (2%)
    pallas_call x1, Pallas kernels, head_shards(): pl.pallas_call(functools.partial(head_kernel, (dp_count, seq_count, capac...  104 us

commit v1 on v0

--- a/solution.py
+++ b/solution.py
@@ -122,6 +122,7 @@
 EXCLUDED = float(1 << 20)
 NT = (((1,), (1,)), ((), ()))
 TN = (((0,), (0,)), ((), ()))
+QUARTERS = 4
 
 
 def head_kernel(
@@ -130,10 +131,14 @@
     k_ref,
     v_ref,
     ids_ref,
-    table_ref,
+    times_ref,
+    w_ref,
     out_ref,
     rows_buf,
     ids_buf,
+    times_buf,
+    w_buf,
+    table_buf,
     place_buf,
     q_slots,
     k_slots,
@@ -142,106 +147,187 @@
     out_buf,
     sem_send,
     sem_recv,
-    sem_out_send,
-    sem_out_recv,
+    sem_side,
+    sweep,
+    line,
 ):
-    dp_count, seq_count, capacity, group = sizes
+    dp_count, seq_count, capacity = sizes
     count = dp_count * seq_count
-    row_count = q_ref.shape[0]
+    slab = count // QUARTERS
+    row_count = out_ref.shape[0]
     slot_count = dp_count * capacity
     me = lax.axis_index("dp") * seq_count + lax.axis_index("seq")
+    quarter = me // slab
+    spot = me % slab
+    inner = (quarter == 1) | (quarter == 2)
+    outer = (quarter == 0) | (quarter == 3)
+    partner = quarter + 1 - 2 * (quarter % 2)
+    across = QUARTERS - 1 - quarter
+    beyond = QUARTERS - 1 - partner
     sources = (k_ref, v_ref, q_ref)
 
     def device_of(index):
         return (index // seq_count, index % seq_count)
 
-    half = count // 2
-
-    def peer(away, shift):
-        return ((me // half + away) % 2) * half + (me % half + shift + half) % half
-
-    def each_peer(visit):
-        @pl.loop(0, half)
-        def _(shift):
-            visit(1, shift)
-
-            @pl.when(shift > 0)
-            def _():
-                visit(0, shift)
+    def mixed_spot(step):
+        total, bit = 0, 1
+        while bit < slab:
+            total = total + (spot // bit + step // bit) % 2 * bit
+            bit *= 2
+        return total
+
+    def at_spot(of_quarter, step):
+        return of_quarter * slab + mixed_spot(step)
 
     def head_columns(index):
         return pl.ds(pl.multiple_of(index * HEAD_DIM, HEAD_DIM), HEAD_DIM)
 
-    def part_copy(part, target, origin):
+    def part_copy(part, target):
         return pltpu.make_async_remote_copy(
             src_ref=sources[part].at[:, head_columns(target)],
-            dst_ref=rows_buf.at[origin, :, pl.ds(part * HEAD_DIM, HEAD_DIM)],
-            send_sem=sem_send.at[part, target],
-            recv_sem=sem_recv.at[part, origin],
+            dst_ref=rows_buf.at[part, me],
+            send_sem=sem_send.at[part],
+            recv_sem=sem_recv.at[part, quarter],
             device_id=device_of(target),
             device_id_type=pl.DeviceIdType.MESH,
         )
 
-    def ids_copy(target, origin):
+    def ids_copy(target):
         return pltpu.make_async_remote_copy(
             src_ref=ids_ref,
-            dst_ref=ids_buf.at[origin],
-            send_sem=sem_send.at[3, target],
-            recv_sem=sem_recv.at[3, origin],
+            dst_ref=ids_buf.at[me],
+            send_sem=sem_send.at[3],
+            recv_sem=sem_recv.at[3, quarter],
             device_id=device_of(target),
             device_id_type=pl.DeviceIdType.MESH,
         )
 
-    def own_copy(part):
-        return pltpu.make_async_copy(
-            sources[part].at[:, head_columns(me)],
-            rows_buf.at[me, :, pl.ds(part * HEAD_DIM, HEAD_DIM)],
-            sem_recv.at[part, me],
-        )
-
-    def out_copy(target, origin):
+    def out_copy(target):
         return pltpu.make_async_remote_copy(
             src_ref=out_buf.at[target],
-            dst_ref=out_ref.at[:, head_columns(origin)],
-            send_sem=sem_out_send.at[target],
-            recv_sem=sem_out_recv.at[origin],
+            dst_ref=out_ref.at[:, head_columns(me)],
+            send_sem=sem_send.at[4],
+            recv_sem=sem_side.at[0],
             device_id=device_of(target),
             device_id_type=pl.DeviceIdType.MESH,
         )
 
     def own_out():
         return pltpu.make_async_copy(
-            out_buf.at[me], out_ref.at[:, head_columns(me)], sem_out_send.at[me]
-        )
+            out_buf.at[me], out_ref.at[:, head_columns(me)], sem_side.at[0]
+        )
+
+    def wait_for(region, sem):
+        pltpu.make_async_copy(region, region, sem).wait()
+
+    def slab_of(of_quarter):
+        return pl.ds(pl.multiple_of(of_quarter * slab, slab), slab)
+
+    def tell(sem, target):
+        pl.semaphore_signal(
+            sem, inc=1, device_id=device_of(target), device_id_type=pl.DeviceIdType.MESH
+        )
+
+    def send_k(target):
+        ids_copy(target).start()
+        part_copy(0, target).start()
+
+    barrier = pltpu.get_barrier_semaphore()
+    pair = min(2, slab)
+    bits = [1 << n for n in range(slab.bit_length() - 1)]
+
+    @pl.when(inner)
+    def _():
+        for step in range(pair):
+            tell(barrier, at_spot(across, step))
+        for step in range(pair):
+            tell(barrier, at_spot(partner, step))
+
+    for bit in bits:
+        tell(barrier, at_spot(quarter, bit))
 
     for part in range(3):
-        own_copy(part).start()
-
-    barrier = pltpu.get_barrier_semaphore()
-
-    def greet(away, shift):
-        pl.semaphore_signal(
-            barrier,
-            inc=1,
-            device_id=device_of(peer(away, shift)),
-            device_id_type=pl.DeviceIdType.MESH,
-        )
-
-    each_peer(greet)
-    pl.semaphore_wait(barrier, count - 1)
-
-    def send_first(away, shift):
-        target = peer(away, shift)
-        ids_copy(target, me).start()
-        part_copy(0, target, me).start()
-
-    each_peer(send_first)
-    for part in (1, 2):
-        each_peer(lambda away, shift: part_copy(part, peer(away, shift), me).start())
-
-    v_slots[:, :, HEAD_DIM:] = jnp.ones(
-        (dp_count, count * capacity, HEAD_DIM), jnp.bfloat16
-    )
+        pltpu.make_async_copy(
+            sources[part].at[:, head_columns(me)], rows_buf.at[part, me], sem_recv.at[part, quarter]
+        ).start()
+    pltpu.make_async_copy(ids_ref, ids_buf.at[me], sem_recv.at[3, quarter]).start()
+    times_copy = pltpu.make_async_copy(times_ref, times_buf, sem_side.at[1])
+    w_copy = pltpu.make_async_copy(w_ref.at[:, head_columns(me)], w_buf, sem_side.at[2])
+    times_copy.start()
+    w_copy.start()
+
+    pl.semaphore_wait(barrier, len(bits) + pair)
+
+    @pl.when(inner)
+    def _():
+        for step in range(pair):
+            send_k(at_spot(across, step))
+
+    for n, bit in enumerate(bits[1:]):
+        tell(sweep.at[n], at_spot(quarter, bit))
+        pl.semaphore_wait(sweep.at[n], 1)
+
+    @pl.when(outer)
+    def _():
+        tell(line.at[0], at_spot(partner, 0))
+        for step in range(1, slab):
+            send_k(at_spot(quarter, step))
+        for step in range(slab):
+            send_k(at_spot(partner, step))
+        pl.semaphore_wait(line.at[0], 1)
+        for step in range(slab):
+            send_k(at_spot(across, step))
+            send_k(at_spot(beyond, step))
+
+    @pl.when(inner)
+    def _():
+        for step in range(pair, slab):
+            send_k(at_spot(across, step))
+        pl.semaphore_wait(line.at[0], 1)
+        tell(line.at[1], at_spot(across, 0))
+        for step in range(1, slab):
+            send_k(at_spot(quarter, step))
+        pl.semaphore_wait(line.at[1], 1)
+        tell(line.at[0], at_spot(partner, 0))
+        for step in range(slab):
+            send_k(at_spot(beyond, step))
+            send_k(at_spot(partner, step))
+
+    def send_part(part):
+        @pl.loop(0, slab)
+        def _(step):
+            part_copy(part, at_spot(across, step)).start()
+            part_copy(part, at_spot(beyond, step)).start()
+            part_copy(part, at_spot(partner, step)).start()
+
+            @pl.when(step > 0)
+            def _():
+                part_copy(part, at_spot(quarter, step)).start()
+
+    send_part(1)
+    send_part(2)
+
+    times_copy.wait()
+    samples = times_buf.shape[1]
+    square = (samples, samples)
+    diagonal = lax.broadcasted_iota(jnp.int32, square, 0) == lax.broadcasted_iota(
+        jnp.int32, square, 1
+    )
+    times = jnp.broadcast_to(times_buf[...].astype(jnp.float32), square)
+    times = jnp.sum(jnp.where(diagonal, times, 0.0), axis=1, keepdims=True)
+    half_freq = FREQ // 2
+    ramp = lax.broadcasted_iota(jnp.int32, (1, half_freq), 1).astype(jnp.float32)
+    angles = times * jnp.exp(-math.log(10000.0) * ramp / half_freq)
+    waves = (jax.nn.silu(wave(angles)).astype(jnp.bfloat16) for wave in (jnp.cos, jnp.sin))
+    w_copy.wait()
+    table_buf[...] = sum(
+        jnp.dot(
+            wave, w_buf[n * half_freq : (n + 1) * half_freq, :], preferred_element_type=jnp.float32
+        )
+        for n, wave in enumerate(waves)
+    )
+
+    v_slots[:, :, HEAD_DIM:] = jnp.ones((dp_count, count * capacity, HEAD_DIM), jnp.bfloat16)
     before = (
         lax.broadcasted_iota(jnp.int32, (row_count, row_count), 0)
         < lax.broadcasted_iota(jnp.int32, (row_count, row_count), 1)
@@ -259,8 +345,7 @@
         )
 
     def placed_part(place, origin, part):
-        rows = rows_buf[origin, :, part * HEAD_DIM : (part + 1) * HEAD_DIM]
-        return jnp.dot(place, rows, preferred_element_type=jnp.float32)
+        return jnp.dot(place, rows_buf[part, origin], preferred_element_type=jnp.float32)
 
     def by_bin(value):
         return value.astype(jnp.bfloat16).reshape((dp_count, capacity, HEAD_DIM))
@@ -289,54 +374,50 @@
         placed = placed_part(place_buf[origin], origin, 1)
         v_slots[:, slots_at(origin), :HEAD_DIM] = by_bin(placed)
 
-    def place_q(origin, inner):
+    def place_q(origin, inner_index):
         place = place_buf[origin]
         own_member = marks_of(place, member_hits(origin))
         q_marks = jnp.where(part_lane, (own_member - 1.0) * EXCLUDED, 0.0)
-        at = slice(inner * capacity, (inner + 1) * capacity)
+        at = slice(inner_index * capacity, (inner_index + 1) * capacity)
         q_slots[:, at, :HEAD_DIM] = by_bin(placed_part(place, origin, 2))
         q_slots[:, at, HEAD_DIM:] = by_bin(q_marks)
 
-    ids_buf[me] = ids_ref[...]
-    own_copy(0).wait()
-    place_k(me)
-
-    def take_k(away, shift):
-        origin = peer(away, -shift)
-        ids_copy(me, origin).wait_recv()
-        part_copy(0, me, origin).wait_recv()
-        place_k(origin)
-
-    each_peer(take_k)
-    own_copy(1).wait()
-    place_v(me)
-
-    def take_v(away, shift):
-        origin = peer(away, -shift)
-        part_copy(1, me, origin).wait_recv()
-        place_v(origin)
-
-    each_peer(take_v)
+    def arrived(part, of_quarter):
+        wait_for(rows_buf.at[part, slab_of(of_quarter)], sem_recv.at[part, of_quarter])
+
+    def turn_quarter(turn):
+        near = jnp.where(turn == 0, quarter, partner)
+        far = jnp.where(turn == 2, across, beyond)
+        return jnp.where(turn < 2, near, far)
+
+    @pl.loop(0, QUARTERS)
+    def _(turn):
+        of_quarter = turn_quarter(turn)
+        wait_for(ids_buf.at[slab_of(of_quarter)], sem_recv.at[3, of_quarter])
+        arrived(0, of_quarter)
+
+        @pl.loop(0, slab)
+        def _(n):
+            place_k(of_quarter * slab + n)
+
+    @pl.loop(0, QUARTERS)
+    def _(turn):
+        of_quarter = turn_quarter(turn)
+        arrived(1, of_quarter)
+
+        @pl.loop(0, slab)
+        def _(n):
+            place_v(of_quarter * slab + n)
 
     exponent_scale = 1.0 / (math.sqrt(HEAD_DIM) * math.log(2.0))
-    group_slots = group * capacity
-
-    def attend_group(away, turn):
-        for inner in range(group):
-            shift = turn * group + inner
-            origin = peer(away, -shift)
-            if away == 0 and inner == 0:
-
-                @pl.when(turn == 0)
-                def _():
-                    own_copy(2).wait()
-
-                @pl.when(turn > 0)
-                def _():
-                    part_copy(2, me, origin).wait_recv()
-            else:
-                part_copy(2, me, origin).wait_recv()
-            place_q(origin, inner)
+    group_slots = slab * capacity
+
+    @pl.loop(0, QUARTERS)
+    def _(turn):
+        of_quarter = turn_quarter(turn)
+        arrived(2, of_quarter)
+        for n in range(slab):
+            place_q(of_quarter * slab + n, n)
 
         @pl.loop(0, dp_count, unroll=8)
         def _(bin_index):
@@ -351,47 +432,34 @@
             factor = jnp.zeros((group_slots, HEAD_DIM), jnp.float32)
             for member in range(SEG_BIN):
                 mark = query[:, HEAD_DIM + member : HEAD_DIM + member + 1].astype(jnp.float32)
-                row = table_ref[pl.ds(bin_index * SEG_BIN + member, 1), :]
+                row = table_buf[pl.ds(bin_index * SEG_BIN + member, 1), :]
                 factor = jnp.where(mark == 0.0, 1.0 + row, factor)
             mixed = (attended.astype(jnp.float32) * factor).astype(jnp.bfloat16)
             group_out[bin_index] = mixed
 
-        for inner in range(group):
-            target = peer(away, -(turn * group + inner))
-            slots = group_out[:, inner * capacity : (inner + 1) * capacity, :].reshape(
+        for n in range(slab):
+            target = of_quarter * slab + n
+            slots = group_out[:, n * capacity : (n + 1) * capacity, :].reshape(
                 (slot_count, HEAD_DIM)
             )
             out_buf[target] = lax.dot_general(
                 place_buf[target], slots, TN, preferred_element_type=jnp.float32
             ).astype(jnp.bfloat16)
-            if away == 0 and inner == 0:
-
-                @pl.when(turn == 0)
-                def _():
-                    own_out().start()
-
-                @pl.when(turn > 0)
-                def _():
-                    out_copy(target, me).start()
-            else:
-                out_copy(target, me).start()
-
-    @pl.loop(0, half // group)
-    def _(turn):
-        attend_group(0, turn)
-        attend_group(1, turn)
-
-    @pl.loop(1, count)
-    def _(step):
-        target = (me + step) % count
-        ids_copy(target, me).wait_send()
-        part_copy(0, target, me).wait_send()
-        part_copy(1, target, me).wait_send()
-        part_copy(2, target, me).wait_send()
-        out_copy(target, me).wait_send()
-        out_copy(me, target).wait_recv()
-
-    own_out().wait()
+
+            @pl.when(target == me)
+            def _():
+                own_out().start()
+
+            @pl.when(target != me)
+            def _():
+                out_copy(target).start()
+
+    others = pl.ds(0, (count - 1) * HEAD_DIM)
+    for part in range(3):
+        wait_for(sources[part].at[:, others], sem_send.at[part])
+    wait_for(ids_buf.at[pl.ds(0, count - 1)], sem_send.at[3])
+    wait_for(out_buf.at[pl.ds(0, count - 1)], sem_send.at[4])
+    wait_for(out_ref, sem_side.at[0])
 
 
 def head_shards(query_rows, key_rows, value_rows, seg_ids, timesteps, w_mod):
@@ -399,44 +467,53 @@
     seq_count = lax.axis_size("seq")
     count = dp_count * seq_count
     row_count, width = query_rows.shape
+    samples = timesteps.shape[0]
     capacity = 2 * row_count // dp_count
-    group = count // 4
-    me = lax.axis_index("dp") * seq_count + lax.axis_index("seq")
-    head_weights = lax.dynamic_slice_in_dim(w_mod, me * HEAD_DIM, HEAD_DIM, 1)
-    scale_table = scale_rows_table(timesteps, head_weights)
-    ids = seg_ids.reshape(1, row_count)
-    vmem = pl.BlockSpec(memory_space=pltpu.VMEM)
+    slab = count // QUARTERS
     anywhere = pl.BlockSpec(memory_space=pl.ANY)
     slots = (dp_count, count * capacity, 2 * HEAD_DIM)
     return pl.pallas_call(
-        functools.partial(head_kernel, (dp_count, seq_count, capacity, group)),
+        functools.partial(head_kernel, (dp_count, seq_count, capacity)),
         out_shape=pltpu.VMEM((row_count, width), jnp.bfloat16),
-        in_specs=[anywhere, anywhere, anywhere, vmem, vmem],
-        out_specs=vmem,
+        in_specs=[anywhere] * 6,
+        out_specs=pl.BlockSpec(memory_space=pltpu.VMEM),
         scratch_shapes=[
-            pltpu.VMEM((count, row_count, 3 * HEAD_DIM), jnp.bfloat16),
+            pltpu.VMEM((3, count, row_count, HEAD_DIM), jnp.bfloat16),
             pltpu.VMEM((count, 1, row_count), jnp.int32),
+            pltpu.VMEM((1, samples), jnp.int32),
+            pltpu.VMEM((FREQ, HEAD_DIM), jnp.bfloat16),
+            pltpu.VMEM((samples, HEAD_DIM), jnp.float32),
             pltpu.VMEM((count, dp_count * capacity, row_count), jnp.bfloat16),
-            pltpu.VMEM((dp_count, group * capacity, 2 * HEAD_DIM), jnp.bfloat16),
+            pltpu.VMEM((dp_count, slab * capacity, 2 * HEAD_DIM), jnp.bfloat16),
             pltpu.VMEM(slots, jnp.bfloat16),
             pltpu.VMEM(slots, jnp.bfloat16),
-            pltpu.VMEM((dp_count, group * capacity, HEAD_DIM), jnp.bfloat16),
+            pltpu.VMEM((dp_count, slab * capacity, HEAD_DIM), jnp.bfloat16),
             pltpu.VMEM((count, row_count, HEAD_DIM), jnp.bfloat16),
-            pltpu.SemaphoreType.DMA((4, count)),
-            pltpu.SemaphoreType.DMA((4, count)),
-            pltpu.SemaphoreType.DMA((count,)),
-            pltpu.SemaphoreType.DMA((count,)),
+            pltpu.SemaphoreType.DMA((5,)),
+            pltpu.SemaphoreType.DMA((4, QUARTERS)),
+            pltpu.SemaphoreType.DMA((3,)),
+            pltpu.SemaphoreType.REGULAR((slab.bit_length(),)),
+            pltpu.SemaphoreType.REGULAR((2,)),
         ],
         compiler_params=pltpu.CompilerParams(
             collective_id=0, has_side_effects=True, vmem_limit_bytes=56 * 1024 * 1024
         ),
-    )(query_rows, key_rows, value_rows, ids, scale_table)
+    )(
+        query_rows,
+        key_rows,
+        value_rows,
+        seg_ids.reshape(1, row_count),
+        timesteps.reshape(1, samples),
+        w_mod,
+    )
 
 
 def shards(query_rows, key_rows, value_rows, seg_ids, timesteps, w_mod):
     count = lax.axis_size("dp") * lax.axis_size("seq")
     whole_heads = query_rows.shape[1] == count * HEAD_DIM
-    body = head_shards if whole_heads else routed_shards
+    slab = count // QUARTERS
+    even_slabs = count == slab * QUARTERS and slab & (slab - 1) == 0 and slab > 1
+    body = head_shards if whole_heads and even_slabs else routed_shards
     return body(query_rows, key_rows, value_rows, seg_ids, timesteps, w_mod)
 
 

time: 108 us -> 105 us (0.972)
  no operation moved by 1% of the time
where the time goes in v1:
time: 105 us
  Pallas kernels  104 us (99%)
    pallas_call x1, Pallas kernels, head_shards(): pl.pallas_call(functools.partial(head_kernel, (dp_count, seq_count, capac...  104 us

profile of v1, /device:TPU:7, one launch (start us, length us, event | category | flops | bytes accessed | tf_op | source)
XLA Modules:
  0.0 105.0 jit_solution(9088614443067782920)
XLA Ops:
  0.0 104.1 %shard_map.64 = bf16[128,4096]{1,0:T(8,128)(2,1)S(1)} custom-call(bf16[128,4096]{1,0:T(8,128)(2,1)} %q_ref.1, bf16[128,4096]{1,0:T(8,128)(2,1)} %k_ref.1, bf16[128,4096]{1,0:T(8,128)(2,1)} %v_ref.1, s32[1,128]{1,0:T(1,128)} %bitcast.2, s32[1,16]{1,0:T(1,128)} %bitcast.3, bf16[256,4096]{1,0:T(8,128)(2,1)} %w_ref.1), custom_call_target="tpu_custom_call" | custom-call | tf_op jit(solution)/shard_map/pallas_call | solution.py:475
  104.1 1.0 copy.8

commit v2 on v1

--- a/solution.py
+++ b/solution.py
@@ -228,9 +228,10 @@
             sem, inc=1, device_id=device_of(target), device_id_type=pl.DeviceIdType.MESH
         )
 
-    def send_k(target):
-        ids_copy(target).start()
-        part_copy(0, target).start()
+    def send(part, target):
+        if part == 0:
+            ids_copy(target).start()
+        part_copy(part, target).start()
 
     barrier = pltpu.get_barrier_semaphore()
     pair = min(2, slab)
@@ -260,52 +261,71 @@
 
     @pl.when(inner)
     def _():
-        for step in range(pair):
-            send_k(at_spot(across, step))
+        for part in range(2):
+            for step in range(pair):
+                send(part, at_spot(across, step))
 
     for n, bit in enumerate(bits[1:]):
         tell(sweep.at[n], at_spot(quarter, bit))
         pl.semaphore_wait(sweep.at[n], 1)
 
+    def send_steps(part, of_quarter, first=0):
+        @pl.loop(first, slab)
+        def _(step):
+            send(part, at_spot(of_quarter, step))
+
     @pl.when(outer)
     def _():
         tell(line.at[0], at_spot(partner, 0))
-        for step in range(1, slab):
-            send_k(at_spot(quarter, step))
-        for step in range(slab):
-            send_k(at_spot(partner, step))
+
+        for part in range(3):
+            send(part, at_spot(partner, 0))
+
+            @pl.loop(1, slab)
+            def _(step):
+                send(part, at_spot(partner, step))
+                send(part, at_spot(quarter, step))
+
         pl.semaphore_wait(line.at[0], 1)
-        for step in range(slab):
-            send_k(at_spot(across, step))
-            send_k(at_spot(beyond, step))
+
+        for part in range(2):
+
+            @pl.loop(0, slab)
+            def _(step):
+                send(part, at_spot(beyond, step))
+                send(part, at_spot(across, step))
+
+        send_steps(2, across)
 
     @pl.when(inner)
     def _():
-        for step in range(pair, slab):
-            send_k(at_spot(across, step))
         pl.semaphore_wait(line.at[0], 1)
         tell(line.at[1], at_spot(across, 0))
-        for step in range(1, slab):
-            send_k(at_spot(quarter, step))
+        for part in range(2):
+            for step in range(pair):
+                send(part, at_spot(partner, step))
+
+            @pl.loop(pair, slab)
+            def _(step):
+                send(part, at_spot(across, step))
+                send(part, at_spot(partner, step))
+
         pl.semaphore_wait(line.at[1], 1)
         tell(line.at[0], at_spot(partner, 0))
-        for step in range(slab):
-            send_k(at_spot(beyond, step))
-            send_k(at_spot(partner, step))
-
-    def send_part(part):
-        @pl.loop(0, slab)
+        for part in range(2):
+            send(part, at_spot(beyond, 0))
+
+            @pl.loop(1, slab)
+            def _(step):
+                send(part, at_spot(beyond, step))
+                send(part, at_spot(quarter, step))
+
+        send(2, at_spot(partner, 0))
+
+        @pl.loop(1, slab)
         def _(step):
-            part_copy(part, at_spot(across, step)).start()
-            part_copy(part, at_spot(beyond, step)).start()
-            part_copy(part, at_spot(partner, step)).start()
-
-            @pl.when(step > 0)
-            def _():
-                part_copy(part, at_spot(quarter, step)).start()
-
-    send_part(1)
-    send_part(2)
+            send(2, at_spot(partner, step))
+            send(2, at_spot(quarter, step))
 
     times_copy.wait()
     samples = times_buf.shape[1]
@@ -385,14 +405,20 @@
     def arrived(part, of_quarter):
         wait_for(rows_buf.at[part, slab_of(of_quarter)], sem_recv.at[part, of_quarter])
 
-    def turn_quarter(turn):
-        near = jnp.where(turn == 0, quarter, partner)
-        far = jnp.where(turn == 2, across, beyond)
-        return jnp.where(turn < 2, near, far)
+    def turn_quarter(turn, order):
+        found = order[-1]
+        for n in range(len(order) - 1):
+            found = jnp.where(turn == n, order[n], found)
+        return found
+
+    far_inner = jnp.where(inner, across, beyond)
+    far_outer = jnp.where(inner, beyond, across)
+    arrivals = (quarter, partner, far_inner, far_outer)
+    queries = (partner, quarter, across, beyond)
 
     @pl.loop(0, QUARTERS)
     def _(turn):
-        of_quarter = turn_quarter(turn)
+        of_quarter = turn_quarter(turn, arrivals)
         wait_for(ids_buf.at[slab_of(of_quarter)], sem_recv.at[3, of_quarter])
         arrived(0, of_quarter)
 
@@ -402,19 +428,24 @@
 
     @pl.loop(0, QUARTERS)
     def _(turn):
-        of_quarter = turn_quarter(turn)
+        of_quarter = turn_quarter(turn, arrivals)
         arrived(1, of_quarter)
 
         @pl.loop(0, slab)
         def _(n):
             place_v(of_quarter * slab + n)
 
+    @pl.when(inner)
+    def _():
+        send_steps(2, across)
+        send_steps(2, beyond)
+
     exponent_scale = 1.0 / (math.sqrt(HEAD_DIM) * math.log(2.0))
     group_slots = slab * capacity
 
     @pl.loop(0, QUARTERS)
     def _(turn):
-        of_quarter = turn_quarter(turn)
+        of_quarter = turn_quarter(turn, queries)
         arrived(2, of_quarter)
         for n in range(slab):
             place_q(of_quarter * slab + n, n)
@@ -453,6 +484,10 @@
             @pl.when(target != me)
             def _():
                 out_copy(target).start()
+
+        @pl.when(outer & (turn == 0))
+        def _():
+            send_steps(2, beyond)
 
     others = pl.ds(0, (count - 1) * HEAD_DIM)
     for part in range(3):

time: 105 us -> 101 us (0.962)
  Pallas kernels: 104 us -> 99.7 us
    pallas_call x1, Pallas kernels: 104 us -> 99.7 us  [head_shards(): pl.pallas_call(functools.partial(head_kernel, (dp_count, seq_count, capac...]
where the time goes in v2:
time: 101 us
  Pallas kernels  99.7 us (99%)
    pallas_call x1, Pallas kernels, head_shards(): pl.pallas_call(functools.partial(head_kernel, (dp_count, seq_count, capac...  99.7 us

profile of v2, /device:TPU:7, one launch (start us, length us, event | category | flops | bytes accessed | tf_op | source)
XLA Modules:
  0.0 100.7 jit_solution(14152989467092542355)
XLA Ops:
  0.0 99.7 %shard_map.64 = bf16[128,4096]{1,0:T(8,128)(2,1)S(1)} custom-call(bf16[128,4096]{1,0:T(8,128)(2,1)} %q_ref.1, bf16[128,4096]{1,0:T(8,128)(2,1)} %k_ref.1, bf16[128,4096]{1,0:T(8,128)(2,1)} %v_ref.1, s32[1,128]{1,0:T(1,128)} %bitcast.2, s32[1,16]{1,0:T(1,128)} %bitcast.3, bf16[256,4096]{1,0:T(8,128)(2,1)} %w_ref.1), custom_call_target="tpu_custom_call" | custom-call | tf_op jit(solution)/shard_map/pallas_call | solution.py:510
  99.7 1.0 copy.8

commit v3 on v2

--- a/solution.py
+++ b/solution.py
@@ -269,63 +269,44 @@
         tell(sweep.at[n], at_spot(quarter, bit))
         pl.semaphore_wait(sweep.at[n], 1)
 
-    def send_steps(part, of_quarter, first=0):
-        @pl.loop(first, slab)
+    def send_rounds(*streams):
+        @pl.loop(0, slab)
         def _(step):
-            send(part, at_spot(of_quarter, step))
+            for part, of_quarter in streams:
+                if of_quarter is quarter:
+                    first = 1
+                elif of_quarter is across and part < 2:
+                    first = jnp.where(inner, pair, 0)
+                else:
+                    first = 0
+
+                @pl.when(step >= first)
+                def _():
+                    send(part, at_spot(of_quarter, step))
 
     @pl.when(outer)
     def _():
         tell(line.at[0], at_spot(partner, 0))
-
-        for part in range(3):
-            send(part, at_spot(partner, 0))
-
-            @pl.loop(1, slab)
-            def _(step):
-                send(part, at_spot(partner, step))
-                send(part, at_spot(quarter, step))
-
+        send_rounds((0, partner), (0, quarter))
+        send_rounds((1, partner), (1, quarter))
+        send_rounds((2, partner), (2, quarter))
         pl.semaphore_wait(line.at[0], 1)
-
-        for part in range(2):
-
-            @pl.loop(0, slab)
-            def _(step):
-                send(part, at_spot(beyond, step))
-                send(part, at_spot(across, step))
-
-        send_steps(2, across)
+        send_rounds((0, beyond), (0, across))
+        send_rounds((1, beyond), (1, across))
+        send_rounds((2, across))
+        send_rounds((2, beyond))
 
     @pl.when(inner)
     def _():
         pl.semaphore_wait(line.at[0], 1)
         tell(line.at[1], at_spot(across, 0))
-        for part in range(2):
-            for step in range(pair):
-                send(part, at_spot(partner, step))
-
-            @pl.loop(pair, slab)
-            def _(step):
-                send(part, at_spot(across, step))
-                send(part, at_spot(partner, step))
-
+        send_rounds((0, across), (0, partner))
+        send_rounds((1, across), (1, partner))
         pl.semaphore_wait(line.at[1], 1)
         tell(line.at[0], at_spot(partner, 0))
-        for part in range(2):
-            send(part, at_spot(beyond, 0))
-
-            @pl.loop(1, slab)
-            def _(step):
-                send(part, at_spot(beyond, step))
-                send(part, at_spot(quarter, step))
-
-        send(2, at_spot(partner, 0))
-
-        @pl.loop(1, slab)
-        def _(step):
-            send(2, at_spot(partner, step))
-            send(2, at_spot(quarter, step))
+        send_rounds((0, beyond), (0, quarter))
+        send_rounds((1, beyond), (1, quarter))
+        send_rounds((2, partner), (2, quarter))
 
     times_copy.wait()
     samples = times_buf.shape[1]
@@ -411,34 +392,43 @@
             found = jnp.where(turn == n, order[n], found)
         return found
 
-    far_inner = jnp.where(inner, across, beyond)
-    far_outer = jnp.where(inner, beyond, across)
-    arrivals = (quarter, partner, far_inner, far_outer)
-    queries = (partner, quarter, across, beyond)
-
-    @pl.loop(0, QUARTERS)
-    def _(turn):
-        of_quarter = turn_quarter(turn, arrivals)
-        wait_for(ids_buf.at[slab_of(of_quarter)], sem_recv.at[3, of_quarter])
-        arrived(0, of_quarter)
-
-        @pl.loop(0, slab)
-        def _(n):
-            place_k(of_quarter * slab + n)
-
-    @pl.loop(0, QUARTERS)
-    def _(turn):
-        of_quarter = turn_quarter(turn, arrivals)
-        arrived(1, of_quarter)
-
-        @pl.loop(0, slab)
-        def _(n):
-            place_v(of_quarter * slab + n)
+    arrivals = (
+        partner,
+        jnp.where(inner, across, quarter),
+        jnp.where(inner, quarter, beyond),
+        jnp.where(inner, beyond, across),
+    )
+    queries = (
+        partner,
+        jnp.where(inner, beyond, across),
+        quarter,
+        jnp.where(inner, across, beyond),
+    )
+
+    @pl.loop(0, 2)
+    def _(stage):
+        @pl.loop(2 * stage, 2 * stage + 2)
+        def _(turn):
+            of_quarter = turn_quarter(turn, arrivals)
+            wait_for(ids_buf.at[slab_of(of_quarter)], sem_recv.at[3, of_quarter])
+            arrived(0, of_quarter)
+
+            @pl.loop(0, slab)
+            def _(n):
+                place_k(of_quarter * slab + n)
+
+        @pl.loop(2 * stage, 2 * stage + 2)
+        def _(turn):
+            of_quarter = turn_quarter(turn, arrivals)
+            arrived(1, of_quarter)
+
+            @pl.loop(0, slab)
+            def _(n):
+                place_v(of_quarter * slab + n)
 
     @pl.when(inner)
     def _():
-        send_steps(2, across)
-        send_steps(2, beyond)
+        send_rounds((2, beyond))
 
     exponent_scale = 1.0 / (math.sqrt(HEAD_DIM) * math.log(2.0))
     group_slots = slab * capacity
@@ -447,8 +437,13 @@
     def _(turn):
         of_quarter = turn_quarter(turn, queries)
         arrived(2, of_quarter)
+
+        @pl.when(inner & (turn == 1))
+        def _():
+            send_rounds((2, across))
+
         for n in range(slab):
-            place_q(of_quarter * slab + n, n)
+            place_q(at_spot(of_quarter, n), n)
 
         @pl.loop(0, dp_count, unroll=8)
         def _(bin_index):
@@ -469,7 +464,7 @@
             group_out[bin_index] = mixed
 
         for n in range(slab):
-            target = of_quarter * slab + n
+            target = at_spot(of_quarter, n)
             slots = group_out[:, n * capacity : (n + 1) * capacity, :].reshape(
                 (slot_count, HEAD_DIM)
             )
@@ -484,10 +479,6 @@
             @pl.when(target != me)
             def _():
                 out_copy(target).start()
-
-        @pl.when(outer & (turn == 0))
-        def _():
-            send_steps(2, beyond)
 
     others = pl.ds(0, (count - 1) * HEAD_DIM)
     for part in range(3):

time: 101 us -> 98 us (0.970)
  the two profiles are of different devices: /device:TPU:7 before, /device:TPU:17 now
where the time goes in v3:
time: 98 us; the launch traced here: 97.9 us
  Pallas kernels  96.9 us (99%)
    pallas_call x1, Pallas kernels, head_shards(): pl.pallas_call(functools.partial(head_kernel, (dp_count, seq_count, capac...  96.9 us

profile of v3, /device:TPU:17, one launch (start us, length us, event | category | flops | bytes accessed | tf_op | source)
XLA Modules:
  0.0 97.9 jit_solution(15558197229226898725)
XLA Ops:
  0.0 96.9 %shard_map.64 = bf16[128,4096]{1,0:T(8,128)(2,1)S(1)} custom-call(bf16[128,4096]{1,0:T(8,128)(2,1)} %q_ref.1, bf16[128,4096]{1,0:T(8,128)(2,1)} %k_ref.1, bf16[128,4096]{1,0:T(8,128)(2,1)} %v_ref.1, s32[1,128]{1,0:T(1,128)} %bitcast.2, s32[1,16]{1,0:T(1,128)} %bitcast.3, bf16[256,4096]{1,0:T(8,128)(2,1)} %w_ref.1), custom_call_target="tpu_custom_call" | custom-call | tf_op jit(solution)/shard_map/pallas_call | solution.py:501
  96.9 1.0 copy.8

commit v4 on v3

--- a/solution.py
+++ b/solution.py
@@ -280,28 +280,28 @@
                 else:
                     first = 0
 
-                @pl.when(step >= first)
+                @pl.when((step >= first) if part < 2 else (slab - 1 - step >= first))
                 def _():
-                    send(part, at_spot(of_quarter, step))
+                    send(part, at_spot(of_quarter, jnp.where(part == 2, slab - 1 - step, step)))
 
     @pl.when(outer)
     def _():
         tell(line.at[0], at_spot(partner, 0))
-        send_rounds((0, partner), (0, quarter))
-        send_rounds((1, partner), (1, quarter))
-        send_rounds((2, partner), (2, quarter))
         pl.semaphore_wait(line.at[0], 1)
-        send_rounds((0, beyond), (0, across))
-        send_rounds((1, beyond), (1, across))
-        send_rounds((2, across))
-        send_rounds((2, beyond))
+        send_rounds((0, across), (0, partner))
+        send_rounds((0, beyond), (0, quarter))
+        send_rounds((1, across), (1, partner))
+        send_rounds((1, beyond), (1, quarter))
+        send_rounds((2, across), (2, partner))
+        send_rounds((2, beyond), (2, quarter))
 
     @pl.when(inner)
     def _():
+        send_rounds((0, across))
         pl.semaphore_wait(line.at[0], 1)
         tell(line.at[1], at_spot(across, 0))
-        send_rounds((0, across), (0, partner))
-        send_rounds((1, across), (1, partner))
+        send_rounds((0, partner), (1, across))
+        send_rounds((1, partner))
         pl.semaphore_wait(line.at[1], 1)
         tell(line.at[0], at_spot(partner, 0))
         send_rounds((0, beyond), (0, quarter))
@@ -443,7 +443,7 @@
             send_rounds((2, across))
 
         for n in range(slab):
-            place_q(at_spot(of_quarter, n), n)
+            place_q(at_spot(of_quarter, slab - 1 - n), n)
 
         @pl.loop(0, dp_count, unroll=8)
         def _(bin_index):
@@ -464,7 +464,7 @@
             group_out[bin_index] = mixed
 
         for n in range(slab):
-            target = at_spot(of_quarter, n)
+            target = at_spot(of_quarter, slab - 1 - n)
             slots = group_out[:, n * capacity : (n + 1) * capacity, :].reshape(
                 (slot_count, HEAD_DIM)
             )

time: 98 us -> 95.6 us (0.976)
  the two profiles are of different devices: /device:TPU:17 before, /device:TPU:9 now
where the time goes in v4:
time: 95.6 us; the launch traced here: 95.4 us
  Pallas kernels  94.4 us (99%)
  local copies, waits for them, and re-layouts  0.97 us (1%)
    pallas_call x1, Pallas kernels, head_shards(): pl.pallas_call(functools.partial(head_kernel, (dp_count, seq_count, capac...  94.4 us

profile of v4, /device:TPU:9, one launch (start us, length us, event | category | flops | bytes accessed | tf_op | source)
XLA Modules:
  0.0 95.4 jit_solution(10004750433719482299)
XLA Ops:
  0.0 94.4 %shard_map.64 = bf16[128,4096]{1,0:T(8,128)(2,1)S(1)} custom-call(bf16[128,4096]{1,0:T(8,128)(2,1)} %q_ref.1, bf16[128,4096]{1,0:T(8,128)(2,1)} %k_ref.1, bf16[128,4096]{1,0:T(8,128)(2,1)} %v_ref.1, s32[1,128]{1,0:T(1,128)} %bitcast.2, s32[1,16]{1,0:T(1,128)} %bitcast.3, bf16[256,4096]{1,0:T(8,128)(2,1)} %w_ref.1), custom_call_target="tpu_custom_call" | custom-call | tf_op jit(solution)/shard_map/pallas_call | solution.py:501
  94.4 1.0 %copy.8 = bf16[128,4096]{1,0:T(8,128)(2,1)} copy(bf16[128,4096]{1,0:T(8,128)(2,1)S(1)} %shard_map.64) | data formatting | bytes 2097152
